TPU v7x, 512 devices: a whole 4x4x16 slice. The times are simulated.
512 devices in a mesh: sx: 32 (over z_hi, y, core), sy: 16 (over x, z_lo).
Axes of the slice: x: 4, y: 4, z: 16 (z_hi: 4, z_lo: 4; z = z_hi * 4 + z_lo), core: 2. Of those that a mesh axis runs over, the one named last changes fastest.
Arguments:
- forward_prop: bfloat16 [2, 2, 12, 12, 64, 4096], P(None, None, None, None, 'sx', 'sy'), may hold values from -0.08984375 to 0.08984375
- backward_prop: bfloat16 [2, 2, 12, 12, 64, 4096], P(None, None, None, None, 'sx', 'sy'), may hold values from -0.08984375 to 0.08984375
- gamma_table: int32 [16, 4, 2], replicated, may hold values from 0 to 3, as said below
- source_site: int32 [3], replicated, may hold values from 0 to 63
- momenta: int32 [32, 3], replicated, may hold values from -8 to 7
Outputs:
- corr: float32 [16, 2, 2, 64, 4096], P(None, None, None, 'sx', 'sy')
- listed: float32 [2, 16, 2, 32], replicated
Inputs may be any that keep to these rules, and one draw needn't show every extreme that they name: For every insertion g, gamma_table[g, 0..3, 0] is a permutation of 0..3; gamma_table[g, s, 1] is the power of i of that entry.
All inputs are finite; a program needn't handle non-finite values.
Results may differ from a plain program's by a relative error of at most 0.0003.
Values sent between devices are 32-bit elements; how exact they have to be, the bound alone decides.
A program may use at most 64 MiB of HBM per device.

v0:
```python
import math
import jax
import jax.numpy as jnp
from jax import lax
from jax.sharding import PartitionSpec as P

L = 64
LZ = 64
HIGHEST = lax.Precision.HIGHEST


def gamma_matrices(gamma_table):
    inserts = gamma_table.shape[0]
    columns = gamma_table[:, :, 0]
    powers = gamma_table[:, :, 1]
    spin_ids = jnp.arange(4, dtype=jnp.int32)
    matches = (columns[:, :, None] == spin_ids[None, None, :]).astype(jnp.float32)
    unit_re = (powers == 0).astype(jnp.float32) - (powers == 2).astype(jnp.float32)
    unit_im = (powers == 1).astype(jnp.float32) - (powers == 3).astype(jnp.float32)
    return (
        (matches * unit_re[:, :, None]).reshape(inserts, 16),
        (matches * unit_im[:, :, None]).reshape(inserts, 16),
    )


def dft_table(length, anchor):
    wavenum = jnp.arange(length, dtype=jnp.int32)
    offsets = jnp.mod(wavenum - anchor, length)
    phase_index = jnp.mod(offsets[:, None] * wavenum[None, :], length)
    angles = 2.0 * math.pi / length * phase_index.astype(jnp.float32)
    return (jnp.cos(angles), -jnp.sin(angles))


def complex_step(real_part, imag_part, table_re, table_im, pattern):
    out_re = jnp.einsum(pattern, real_part, table_re, precision=HIGHEST) - jnp.einsum(
        pattern, imag_part, table_im, precision=HIGHEST
    )
    out_im = jnp.einsum(pattern, real_part, table_im, precision=HIGHEST) + jnp.einsum(
        pattern, imag_part, table_re, precision=HIGHEST
    )
    return (out_re, out_im)


def transform(fields, source_site):
    table_re, table_im = dft_table(fields.shape[4], source_site[2])
    along_z = jnp.stack(
        complex_step(fields[:, 0], fields[:, 1], table_re, table_im, "nabz,zk->nabk"), 1
    )
    depth_share = along_z.shape[4] // lax.axis_size("sy")
    first_depth = lax.axis_index("sy") * depth_share
    length_y = along_z.shape[3] * lax.axis_size("sy")
    full_re, full_im = dft_table(length_y, source_site[1])
    part = lax.dynamic_slice_in_dim(
        lax.all_gather(along_z, "sy", axis=3, tiled=True), first_depth, depth_share, 4
    )
    step_re, step_im = complex_step(part[:, 0], part[:, 1], full_re, full_im, "nayc,yk->nakc")
    along_y = jnp.stack([step_re, step_im], 1)
    arrived = lax.all_to_all(along_y, "sx", split_axis=3, concat_axis=2, tiled=True)
    table_re, table_im = dft_table(arrived.shape[2], source_site[0])
    along_x = complex_step(arrived[:, 0], arrived[:, 1], table_re, table_im, "nxbc,xk->nbck")
    return jnp.stack(along_x, 1)


def apply_gammas(mat_re, mat_im, real_part, imag_part):
    extent = real_part.shape
    flat_re = real_part.reshape(extent[0], -1)
    flat_im = imag_part.reshape(extent[0], -1)
    out_re = jnp.dot(mat_re, flat_re, precision=HIGHEST) - jnp.dot(
        mat_im, flat_im, precision=HIGHEST
    )
    out_im = jnp.dot(mat_re, flat_im, precision=HIGHEST) + jnp.dot(
        mat_im, flat_re, precision=HIGHEST
    )
    return (out_re.reshape(extent), out_im.reshape(extent))


def project_sites(fields, source_site, momenta, rows_x, rows_y, length, depth):
    coord_x = lax.axis_index("sx") * rows_x + jnp.arange(rows_x, dtype=jnp.int32) - source_site[0]
    coord_y = lax.axis_index("sy") * rows_y + jnp.arange(rows_y, dtype=jnp.int32) - source_site[1]
    coord_z = jnp.arange(depth, dtype=jnp.int32) - source_site[2]
    part_x = jnp.mod(momenta[:, 0:1] * coord_x[None, :], length)
    part_y = jnp.mod(momenta[:, 1:2] * coord_y[None, :], length)
    part_z = jnp.mod(momenta[:, 2:3] * coord_z[None, :], depth)
    plane = jnp.mod(part_x[:, :, None] + part_y[:, None, :], length).astype(jnp.float32)
    angles = (
        2.0 * math.pi / length * plane[:, :, :, None]
        + 2.0 * math.pi / depth * part_z.astype(jnp.float32)[:, None, None, :]
    )
    angles = angles.reshape(momenta.shape[0], -1)
    cosine = jnp.cos(angles)
    sine = jnp.sin(angles)
    field_re = fields[:, 0].reshape(fields.shape[0], -1)
    field_im = fields[:, 1].reshape(fields.shape[0], -1)
    local_re = jnp.dot(field_re, cosine.T, precision=HIGHEST) + jnp.dot(
        field_im, sine.T, precision=HIGHEST
    )
    local_im = jnp.dot(field_im, cosine.T, precision=HIGHEST) - jnp.dot(
        field_re, sine.T, precision=HIGHEST
    )
    return (local_re, local_im)


def body(forward_prop, backward_prop, gamma_table, source_site, momenta):
    slices = forward_prop.shape[0]
    rows_x = forward_prop.shape[4]
    rows_y = backward_prop.shape[5] // LZ
    inserts = gamma_table.shape[0]
    forward = forward_prop.reshape(slices, 2, 4, 3, 12, -1)
    backward = backward_prop.reshape(slices, 2, 4, 3, 12, -1)
    pattern = "tscjn,tucjn->sutn"
    pair_re = jnp.einsum(
        pattern, backward[:, 0], forward[:, 0], preferred_element_type=jnp.float32
    ) + jnp.einsum(pattern, backward[:, 1], forward[:, 1], preferred_element_type=jnp.float32)
    pair_im = jnp.einsum(
        pattern, backward[:, 0], forward[:, 1], preferred_element_type=jnp.float32
    ) - jnp.einsum(pattern, backward[:, 1], forward[:, 0], preferred_element_type=jnp.float32)
    pair_re = pair_re.reshape(16, slices, -1)
    pair_im = pair_im.reshape(16, slices, -1)
    mat_re, mat_im = gamma_matrices(gamma_table)
    field_re, field_im = apply_gammas(mat_re, mat_im, pair_re, pair_im)
    fields = jnp.stack([field_re, field_im], 2).reshape(inserts * slices, 2, rows_x, rows_y, LZ)
    spectrum = transform(fields, source_site)
    local_re, local_im = project_sites(fields, source_site, momenta, rows_x, rows_y, L, LZ)
    listed_re, listed_im = lax.psum((local_re, local_im), ("sx", "sy"))
    listed_re = listed_re.reshape(inserts, slices, -1)
    listed_im = listed_im.reshape(inserts, slices, -1)
    corr_re = spectrum[:, 0].reshape(inserts, slices, spectrum.shape[2], -1)
    corr_im = spectrum[:, 1].reshape(inserts, slices, spectrum.shape[2], -1)
    return (jnp.stack([corr_re, corr_im], 2), jnp.stack([listed_re, listed_im], 0))


def solution(mesh):
    placed = (
        P(None, None, None, None, "sx", "sy"),
        P(None, None, None, None, "sx", "sy"),
        P(),
        P(),
        P(),
    )
    return jax.shard_map(
        body,
        mesh=mesh,
        in_specs=placed,
        out_specs=(P(None, None, None, "sx", "sy"), P()),
        check_vma=False,
    )
```

profile of v0, /device:TPU:1, one launch (start us, length us, event | category | flops | bytes accessed | tf_op | source)
XLA Modules:
  0.0 323.4 jit_solution(12954592644119887692)
XLA Ops:
  7.2 0.7 fusion.92
  7.9 2.1 reshape.371
  10.0 0.8 fusion.144
  10.9 4.5 %copy.82 = bf16[2,1,4,3,12,512]{4,2,3,5,0,1:T(4,128)(2,1)S(1)} copy(bf16[2,1,4,3,12,512]{5,4,3,2,1,0:T(8,128)(2,1)} %get-tuple-element.11) | data formatting | bytes 589824
  15.3 2.8 reshape.372
  18.1 2.1 fusion.145
  20.2 5.3 %copy.83 = bf16[2,1,4,3,12,512]{4,2,3,5,0,1:T(4,128)(2,1)} copy(bf16[2,1,4,3,12,512]{5,4,3,2,1,0:T(8,128)(2,1)} %get-tuple-element.13) | data formatting | bytes 589824
  25.4 3.8 %copy.80 = bf16[2,1,4,3,12,512]{4,2,3,5,0,1:T(4,128)(2,1)} copy(bf16[2,1,4,3,12,512]{5,4,3,2,1,0:T(8,128)(2,1)S(1)} %get-tuple-element.10) | data formatting | bytes 589824
  29.2 5.3 %copy.81 = bf16[2,1,4,3,12,512]{4,2,3,5,0,1:T(4,128)(2,1)} copy(bf16[2,1,4,3,12,512]{5,4,3,2,1,0:T(8,128)(2,1)} %get-tuple-element.12) | data formatting | bytes 589824
  34.5 5.6 %fusion.2 = f32[2,512,4,4,1]{3,2,4,1,0:T(4,128)S(1)} fusion(bf16[2,1,4,3,12,512]{4,2,3,5,0,1:T(4,128)(2,1)} %copy.83, bf16[2,1,4,3,12,512]{4,2,3,5,0,1:T(4,128)(2,1)S(1)} %copy.82), kind=kOutput, calls=%fused_computation.2 | convolution fusion | flops 1179648 | bytes 655360 | tf_op jit(solution)/shard_map/tscjn,tucjn->sutn/dot_general | solution.py:113
  40.2 5.0 %fusion = f32[2,512,4,4,1]{3,2,4,1,0:T(4,128)} fusion(bf16[2,1,4,3,12,512]{4,2,3,5,0,1:T(4,128)(2,1)S(1)} %copy-done.1, bf16[2,1,4,3,12,512]{4,2,3,5,0,1:T(4,128)(2,1)S(1)} %copy-done.2), kind=kOutput, calls=%fused_computation | convolution fusion | flops 1179648 | bytes 655360 | tf_op jit(solution)/shard_map/tscjn,tucjn->sutn/dot_general | solution.py:116
  45.2 3.7 %fusion.13 = f32[4,4,2,512]{0,1,3,2:T(4,128)} fusion(f32[2,512,4,4,1]{3,2,4,1,0:T(4,128)S(1)} %fusion.2, bf16[2,1,4,3,12,512]{4,2,3,5,0,1:T(4,128)(2,1)S(1)} %copy-done, bf16[2,1,4,3,12,512]{4,2,3,5,0,1:T(4,128)(2,1)S(1)} %copy-done.2), kind=kOutput, calls=%fused_computation.17 | convolution fusion | flops 1196032 | bytes 720896 | tf_op jit(solution)/shard_map/tscjn,tucjn->sutn/dot_general | solution.py:111
  48.8 2.1 copy.48
  51.0 7.5 %fusion.12 = f32[4,4,2,512]{0,1,3,2:T(4,128)} fusion(f32[2,512,4,4,1]{3,2,4,1,0:T(4,128)} %fusion, bf16[2,1,4,3,12,512]{4,2,3,5,0,1:T(4,128)(2,1)} %copy.81, bf16[2,1,4,3,12,512]{4,2,3,5,0,1:T(4,128)(2,1)S(1)} %copy.82), kind=kOutput, calls=%fused_computation.15 | convolution fusion | flops 1196032 | bytes 720896 | tf_op jit(solution)/shard_map/tscjn,tucjn->sutn/dot_general | solution.py:114
  58.5 1.9 copy.49
  60.5 0.7 fusion.146
  61.1 0.3 fusion.147
  61.4 0.3 fusion.148
  61.6 0.3 convolution_subtract_fusion.3
  61.9 0.1 squeeze.52
  62.0 1.3 and_select_fusion.1
  63.3 0.5 fusion.32
  63.8 0.5 fusion.30
  64.2 0.3 convolution_add_fusion.3
  64.5 0.1 squeeze.54
  64.6 0.5 fusion.25
  65.1 0.5 fusion.24
  65.5 0.7 pad_maximum_fusion
  66.3 0.6 iota_subtract_fusion
  67.0 0.7 add_subtract_fusion.1
  67.6 0.7 add_subtract_fusion
  68.6 0.1 fusion.45
  68.7 1.1 add_sine_fusion
  69.8 0.1 cos.29
  70.0 0.7 and_select_fusion.3
  70.7 0.2 fusion.149
  70.9 0.2 convolution_add_fusion.4
  71.1 107.5 %all-gather.2.cloned.1.call-done = f32[32,2,2,64,64]{4,0,3,2,1:T(8,128)} async-done(((f32[32,2,2,4,64]{4,0,3,2,1:T(8,128)}), f32[32,2,2,64,64]{4,0,3,2,1:T(8,128)}) %all-gather.2.cloned.1.call-update) | async-done | bytes 2097168 | tf_op jit(solution)/shard_map/all_gather | solution.py:54
  178.6 4.7 %dynamic-slice_bitcast_fusion = (f32[32,2,64,4]{3,0,2,1:T(8,128)S(1)}, f32[32,2,64,4]{3,0,2,1:T(8,128)}) fusion(f32[32,2,2,64,64]{4,0,3,2,1:T(8,128)} %all-gather.2.cloned.1.call-done, s32[]{:T(128)S(6)} %add.213, s32[]{:T(128)S(6)} %select_n.88), kind=kLoop, calls=%fused_computation.12 | loop fusion | bytes 262152 | tf_op jit(solution)/shard_map/squeeze | solution.py:56
  183.3 2.6 copy.54
  186.0 0.5 fusion.51
  186.4 0.5 fusion.53
  186.9 1.2 copy.55
  188.1 0.5 fusion.23
  188.5 0.5 fusion.22
  189.0 0.3 copy.58
  189.4 1.0 reshape.373
  190.4 13.0 %all-to-all-start = ((f32[32,1,1024]{2,1,0:T(1,128)}), f32[32,1,1024]{2,1,0:T(1,128)S(1)}, u32[]{:S(2)}, u32[]{:S(2)}) async-start(f32[32,1,1024]{2,1,0:T(1,128)} %reshape.373), calls=%async_computation | async-start | bytes 262144 | tf_op jit(solution)/shard_map/all_to_all | solution.py:58
  203.4 0.2 fusion.150
  203.6 0.2 convolution_subtract_fusion.4
  203.8 106.2 %all-reduce = (f32[1,16,2,32]{3,2,1,0:T(2,128)S(1)}, f32[1,16,2,32]{3,2,1,0:T(2,128)S(1)}) all-reduce(f32[1,16,2,32]{3,2,1,0:T(2,128)S(1)} %bitcast.184, f32[1,16,2,32]{3,2,1,0:T(2,128)S(1)} %bitcast.183), channel_id=1, replica_groups=mesh['sx'=32,'sy'=16] {'sx','sy'}, use_global_device_ids=true, to_apply=%region_1.2 | all-reduce | flops 2048 | bytes 16384 | tf_op jit(solution)/shard_map/psum | solution.py:124
  309.9 0.6 pad_maximum_fusion.3
  310.6 0.5 broadcast.522
  311.1 0.9 reduce
  312.0 0.3 reshape.374
  312.3 0.2 copy.59
  312.5 0.4 copy.60
  312.9 0.6 fusion.27
  313.5 0.6 fusion.26
  314.1 0.6 convolution_subtract_fusion.2
  314.9 0.1 stack_reshape_squeeze_stack.6
  315.0 0.6 convolution_add_fusion.2
  315.7 0.1 stack_reshape_squeeze_stack.7
  315.9 0.7 copy.65
  (29 shorter events, 0.8 us)
Async XLA Ops:
  7.2 171.4 %all-gather.2.cloned.1.call-start = ((), (), s32[]{:S(2)}) async-start(), calls=%async_computation.1 | async-start | bytes 4456448 | tf_op jit(solution)/shard_map/all_gather | solution.py:54
  34.5 5.6 %copy-start.1 = (bf16[2,1,4,3,12,512]{4,2,3,5,0,1:T(4,128)(2,1)S(1)}, bf16[2,1,4,3,12,512]{4,2,3,5,0,1:T(4,128)(2,1)}, u32[]{:S(2)}) copy-start(bf16[2,1,4,3,12,512]{4,2,3,5,0,1:T(4,128)(2,1)} %copy.83) | copy-start | bytes 884740
  34.5 5.6 %copy-start.2 = (bf16[2,1,4,3,12,512]{4,2,3,5,0,1:T(4,128)(2,1)S(1)}, bf16[2,1,4,3,12,512]{4,2,3,5,0,1:T(4,128)(2,1)}, u32[]{:S(2)}) copy-start(bf16[2,1,4,3,12,512]{4,2,3,5,0,1:T(4,128)(2,1)} %copy.80) | copy-start | bytes 884740
  40.2 5.0 %copy-start = (bf16[2,1,4,3,12,512]{4,2,3,5,0,1:T(4,128)(2,1)S(1)}, bf16[2,1,4,3,12,512]{4,2,3,5,0,1:T(4,128)(2,1)}, u32[]{:S(2)}) copy-start(bf16[2,1,4,3,12,512]{4,2,3,5,0,1:T(4,128)(2,1)} %copy.81) | copy-start | bytes 884740
  50.9 9.5 %copy-start.3 = (s32[3]{0:T(128)S(1)}, s32[3]{0:T(128)}, u32[]{:S(2)}) copy-start(s32[3]{0:T(128)} %param.8) | copy-start | bytes 40
  50.9 10.2 %slice-start = ((s32[16,4,2]{0,2,1:T(2,128)}), s32[16,4,1]{0,2,1:T(1,128)S(1)}, s32[]{:S(2)}) async-start(s32[16,4,2]{0,2,1:T(2,128)} %param.7), calls=%async_computation.2 | async-start | bytes 4096 | tf_op jit(solution)/shard_map/slice | solution.py:14
  58.5 9.8 %copy-start.4 = (s32[32,3]{0,1:T(4,128)S(1)}, s32[32,3]{0,1:T(4,128)}, u32[]{:S(2)}) copy-start(s32[32,3]{0,1:T(4,128)} %param.9) | copy-start | bytes 1156
  190.4 120.2 %all-to-all-start = ((f32[32,1,1024]{2,1,0:T(1,128)}), f32[32,1,1024]{2,1,0:T(1,128)S(1)}, u32[]{:S(2)}, u32[]{:S(2)}) async-start(f32[32,1,1024]{2,1,0:T(1,128)} %reshape.373), calls=%async_computation | async-start | bytes 262144 | tf_op jit(solution)/shard_map/all_to_all | solution.py:58
Sparse Core Ops, SparseCore 0:
  66.4 112.1 all-gather.1
where the time goes:
time: 325 us; the launch traced here: 323 us
  waiting for transfers between devices  108 us (33%)
  blocking collectives  106 us (33%)
  local copies, waits for them, and re-layouts  44.1 us (14%)
  matrix products  29.7 us (9%)
  between operations  14.4 us (4%)
  starting transfers between devices  13 us (4%)
  other arithmetic  8.45 us (3%)
    all_gather x1, waiting for transfers between devices, transform(): lax.all_gather(along_z, 'sy', axis=3, tiled=True)  107 us
    psum x1, blocking collectives, body(): listed_re, listed_im = lax.psum((local_re, local_im), ('sx', 'sy'))  106 us
    unnamed x19, local copies, waits for them, and re-layouts  20.8 us
    all_to_all x1, starting transfers between devices, transform(): lax.all_to_all(along_y, 'sx', split_axis=3, concat_axis=2, tiled=True)  13 us
    dot_general x1, matrix products, body(): jnp.einsum(pattern, backward[:, 0], forward[:, 1], preferred_element_type...  7.53 us
  transfers between devices with their start and end apart: 2, of which 1 were waited for; matrix products, arithmetic and copies ran while one was open for 2% of the time, Pallas kernels for 0%

commit v1 on v0

--- a/solution.py
+++ b/solution.py
@@ -121,7 +121,7 @@
     fields = jnp.stack([field_re, field_im], 2).reshape(inserts * slices, 2, rows_x, rows_y, LZ)
     spectrum = transform(fields, source_site)
     local_re, local_im = project_sites(fields, source_site, momenta, rows_x, rows_y, L, LZ)
-    listed_re, listed_im = lax.psum((local_re, local_im), ("sx", "sy"))
+    listed_re, listed_im = lax.psum(lax.psum((local_re, local_im), "sy"), "sx")
     listed_re = listed_re.reshape(inserts, slices, -1)
     listed_im = listed_im.reshape(inserts, slices, -1)
     corr_re = spectrum[:, 0].reshape(inserts, slices, spectrum.shape[2], -1)

time: 325 us -> 461 us (1.42); the launches traced: 323 us -> 454 us
  blocking collectives: 106 us -> 237 us
    psum x1 -> x2, blocking collectives: 106 us -> 237 us  [body(): listed_re, listed_im = lax.psum(lax.psum((local_re, local_im), 'sy'), 'sx')]
  transfers between devices with their start and end apart: 2 -> 2, of which waited for: 1 -> 1; matrix products, arithmetic and copies ran while one was open for 2% -> 1% of each run, Pallas kernels for 0% -> 0%
where the time goes in v1:
time: 461 us; the launch traced here: 454 us
  blocking collectives  237 us (51%)
  waiting for transfers between devices  108 us (23%)
  local copies, waits for them, and re-layouts  44.1 us (10%)
  matrix products  29.8 us (6%)
  between operations  14.4 us (3%)
  starting transfers between devices  13 us (3%)
  other arithmetic  8.31 us (2%)
    psum x2, blocking collectives, body(): listed_re, listed_im = lax.psum(lax.psum((local_re, local_im), 'sy'), 'sx')  237 us
    all_gather x1, waiting for transfers between devices, transform(): lax.all_gather(along_z, 'sy', axis=3, tiled=True)  108 us
    unnamed x19, local copies, waits for them, and re-layouts  20.8 us
    all_to_all x1, starting transfers between devices, transform(): lax.all_to_all(along_y, 'sx', split_axis=3, concat_axis=2, tiled=True)  13 us
  transfers between devices with their start and end apart: 2, of which 1 were waited for; matrix products, arithmetic and copies ran while one was open for 1% of the time, Pallas kernels for 0%

profile of v1, /device:TPU:1, one launch (start us, length us, event | category | flops | bytes accessed | tf_op | source)
XLA Modules:
  0.0 454.5 jit_solution(13888553859849619301)
XLA Ops:
  7.2 0.7 fusion.92
  7.9 2.1 reshape.371
  10.0 0.8 fusion.144
  10.8 4.5 copy.82
  15.3 2.8 reshape.372
  18.1 2.1 fusion.145
  20.2 5.3 %copy.83 = bf16[2,1,4,3,12,512]{4,2,3,5,0,1:T(4,128)(2,1)} copy(bf16[2,1,4,3,12,512]{5,4,3,2,1,0:T(8,128)(2,1)} %get-tuple-element.15) | data formatting | bytes 589824
  25.5 3.8 copy.80
  29.3 5.3 %copy.81 = bf16[2,1,4,3,12,512]{4,2,3,5,0,1:T(4,128)(2,1)} copy(bf16[2,1,4,3,12,512]{5,4,3,2,1,0:T(8,128)(2,1)} %get-tuple-element.14) | data formatting | bytes 589824
  34.6 5.6 %fusion.2 = f32[2,512,4,4,1]{3,2,4,1,0:T(4,128)S(1)} fusion(bf16[2,1,4,3,12,512]{4,2,3,5,0,1:T(4,128)(2,1)} %copy.83, bf16[2,1,4,3,12,512]{4,2,3,5,0,1:T(4,128)(2,1)S(1)} %copy.82), kind=kOutput, calls=%fused_computation.2 | convolution fusion | flops 1179648 | bytes 655360 | tf_op jit(solution)/shard_map/tscjn,tucjn->sutn/dot_general | solution.py:113
  40.2 5.0 %fusion = f32[2,512,4,4,1]{3,2,4,1,0:T(4,128)} fusion(bf16[2,1,4,3,12,512]{4,2,3,5,0,1:T(4,128)(2,1)S(1)} %copy-done.1, bf16[2,1,4,3,12,512]{4,2,3,5,0,1:T(4,128)(2,1)S(1)} %copy-done.2), kind=kOutput, calls=%fused_computation | convolution fusion | flops 1179648 | bytes 655360 | tf_op jit(solution)/shard_map/tscjn,tucjn->sutn/dot_general | solution.py:116
  45.2 3.7 fusion.13
  48.9 2.1 copy.48
  51.0 7.5 %fusion.12 = f32[4,4,2,512]{0,1,3,2:T(4,128)} fusion(f32[2,512,4,4,1]{3,2,4,1,0:T(4,128)} %fusion, bf16[2,1,4,3,12,512]{4,2,3,5,0,1:T(4,128)(2,1)} %copy.81, bf16[2,1,4,3,12,512]{4,2,3,5,0,1:T(4,128)(2,1)S(1)} %copy.82), kind=kOutput, calls=%fused_computation.15 | convolution fusion | flops 1196032 | bytes 720896 | tf_op jit(solution)/shard_map/tscjn,tucjn->sutn/dot_general | solution.py:114
  58.6 1.9 copy.49
  60.5 0.6 fusion.146
  61.1 0.3 fusion.147
  61.4 0.3 fusion.148
  61.6 0.3 convolution_subtract_fusion.3
  61.9 0.1 squeeze.52
  62.0 1.2 and_select_fusion.1
  63.2 0.5 fusion.32
  63.7 0.5 fusion.30
  64.2 0.3 convolution_add_fusion.3
  64.4 0.1 squeeze.54
  64.5 0.5 fusion.25
  65.0 0.5 fusion.24
  65.5 0.7 pad_maximum_fusion
  66.3 0.6 iota_subtract_fusion
  66.8 0.7 add_subtract_fusion.1
  67.5 0.7 add_subtract_fusion
  68.4 0.1 fusion.45
  68.6 1.1 add_sine_fusion
  69.9 0.7 and_select_fusion.3
  70.6 0.2 fusion.149
  70.8 0.2 convolution_add_fusion.4
  71.0 107.6 %all-gather.2.cloned.1.call-done = f32[32,2,2,64,64]{4,0,3,2,1:T(8,128)} async-done(((f32[32,2,2,4,64]{4,0,3,2,1:T(8,128)}), f32[32,2,2,64,64]{4,0,3,2,1:T(8,128)}) %all-gather.2.cloned.1.call-update) | async-done | bytes 2097168 | tf_op jit(solution)/shard_map/all_gather | solution.py:54
  178.6 4.7 %dynamic-slice_bitcast_fusion = (f32[32,2,64,4]{3,0,2,1:T(8,128)S(1)}, f32[32,2,64,4]{3,0,2,1:T(8,128)}) fusion(f32[32,2,2,64,64]{4,0,3,2,1:T(8,128)} %all-gather.2.cloned.1.call-done, s32[]{:T(128)S(6)} %add.217, s32[]{:T(128)S(6)} %select_n.88), kind=kLoop, calls=%fused_computation.12 | loop fusion | bytes 262152 | tf_op jit(solution)/shard_map/squeeze | solution.py:56
  183.2 2.6 copy.54
  185.9 0.5 fusion.51
  186.3 0.5 fusion.53
  186.8 1.2 copy.55
  188.0 0.5 fusion.23
  188.5 0.5 fusion.22
  188.9 0.3 copy.58
  189.3 1.0 reshape.373
  190.3 13.0 %all-to-all-start = ((f32[32,1,1024]{2,1,0:T(1,128)}), f32[32,1,1024]{2,1,0:T(1,128)S(1)}, u32[]{:S(2)}, u32[]{:S(2)}) async-start(f32[32,1,1024]{2,1,0:T(1,128)} %reshape.373), calls=%async_computation | async-start | bytes 262144 | tf_op jit(solution)/shard_map/all_to_all | solution.py:58
  203.3 0.2 fusion.150
  203.5 0.2 convolution_subtract_fusion.4
  203.7 64.9 %all-reduce.1 = (f32[32,32]{1,0:T(8,128)S(1)}, f32[32,32]{1,0:T(8,128)S(1)}) all-reduce(f32[32,32]{1,0:T(8,128)S(1)} %convolution_subtract_fusion.4, f32[32,32]{1,0:T(8,128)S(1)} %convolution_add_fusion.4), channel_id=1, replica_groups=mesh['sx'=32,'sy'=16] {'sy'}, use_global_device_ids=true, to_apply=%region_2.3 | all-reduce | flops 2048 | bytes 16384 | tf_op jit(solution)/shard_map/psum | solution.py:124
  268.6 172.4 %all-reduce = (f32[1,16,2,32]{3,2,1,0:T(2,128)S(1)}, f32[1,16,2,32]{3,2,1,0:T(2,128)S(1)}) all-reduce(f32[1,16,2,32]{3,2,1,0:T(2,128)S(1)} %bitcast.183, f32[1,16,2,32]{3,2,1,0:T(2,128)S(1)} %bitcast.184), channel_id=1, replica_groups=mesh['sx'=32,'sy'=16] {'sx'}, use_global_device_ids=true, to_apply=%region_3.4 | all-reduce | flops 2048 | bytes 16384 | tf_op jit(solution)/shard_map/psum | solution.py:124
  440.9 0.6 pad_maximum_fusion.3
  441.6 0.5 broadcast.522
  442.1 0.9 reduce
  443.1 0.3 reshape.374
  443.3 0.2 copy.59
  443.5 0.4 copy.60
  443.9 0.6 fusion.27
  444.5 0.6 fusion.26
  445.2 0.6 convolution_subtract_fusion.2
  445.9 0.1 stack_reshape_squeeze_stack.6
  446.0 0.6 convolution_add_fusion.2
  446.7 0.1 stack_reshape_squeeze_stack.7
  446.9 0.7 copy.65
  (30 shorter events, 0.9 us)
Async XLA Ops:
  7.2 171.4 %all-gather.2.cloned.1.call-start = ((), (), s32[]{:S(2)}) async-start(), calls=%async_computation.1 | async-start | bytes 4456448 | tf_op jit(solution)/shard_map/all_gather | solution.py:54
  34.5 5.6 %copy-start.1 = (bf16[2,1,4,3,12,512]{4,2,3,5,0,1:T(4,128)(2,1)S(1)}, bf16[2,1,4,3,12,512]{4,2,3,5,0,1:T(4,128)(2,1)}, u32[]{:S(2)}) copy-start(bf16[2,1,4,3,12,512]{4,2,3,5,0,1:T(4,128)(2,1)} %copy.83) | copy-start | bytes 884740
  34.6 5.6 %copy-start.2 = (bf16[2,1,4,3,12,512]{4,2,3,5,0,1:T(4,128)(2,1)S(1)}, bf16[2,1,4,3,12,512]{4,2,3,5,0,1:T(4,128)(2,1)}, u32[]{:S(2)}) copy-start(bf16[2,1,4,3,12,512]{4,2,3,5,0,1:T(4,128)(2,1)} %copy.80) | copy-start | bytes 884740
  40.2 5.0 %copy-start = (bf16[2,1,4,3,12,512]{4,2,3,5,0,1:T(4,128)(2,1)S(1)}, bf16[2,1,4,3,12,512]{4,2,3,5,0,1:T(4,128)(2,1)}, u32[]{:S(2)}) copy-start(bf16[2,1,4,3,12,512]{4,2,3,5,0,1:T(4,128)(2,1)} %copy.81) | copy-start | bytes 884740
  51.0 9.5 %copy-start.3 = (s32[3]{0:T(128)S(1)}, s32[3]{0:T(128)}, u32[]{:S(2)}) copy-start(s32[3]{0:T(128)} %param.8) | copy-start | bytes 40
  51.0 10.1 %slice-start = ((s32[16,4,2]{0,2,1:T(2,128)}), s32[16,4,1]{0,2,1:T(1,128)S(1)}, s32[]{:S(2)}) async-start(s32[16,4,2]{0,2,1:T(2,128)} %param.7), calls=%async_computation.2 | async-start | bytes 4096 | tf_op jit(solution)/shard_map/slice | solution.py:14
  58.6 9.6 %copy-start.4 = (s32[32,3]{0,1:T(4,128)S(1)}, s32[32,3]{0,1:T(4,128)}, u32[]{:S(2)}) copy-start(s32[32,3]{0,1:T(4,128)} %param.9) | copy-start | bytes 1156
  190.3 251.3 %all-to-all-start = ((f32[32,1,1024]{2,1,0:T(1,128)}), f32[32,1,1024]{2,1,0:T(1,128)S(1)}, u32[]{:S(2)}, u32[]{:S(2)}) async-start(f32[32,1,1024]{2,1,0:T(1,128)} %reshape.373), calls=%async_computation | async-start | bytes 262144 | tf_op jit(solution)/shard_map/all_to_all | solution.py:58
Sparse Core Ops, SparseCore 0:
  66.3 112.1 all-gather.1
